TPU v7x, 256 devices: a whole 4x4x8 slice. The times are simulated.
256 devices in a mesh: segment: 4 (over y), mp: 16 (over z, core), dp: 4 (over x).
Axes of the slice: x: 4, y: 4, z: 8, core: 2. Of those that a mesh axis runs over, the one named last changes fastest.
Arguments:
- text_rows: bfloat16 [4, 512, 1024], P(None, 'dp'), may hold values from -6 to 6
- durations: int32 [4, 4, 128], P(None, 'dp'), may hold values from 1 to 16, 512 in all within a row
- unit_targets: int32 [4, 2048], P(None, 'dp'), may hold values from 0 to 9999
- w_in: bfloat16 [4, 1024, 8192], P('segment', None, 'mp'), may hold values from -0.1875 to 0.1875
- w_out: bfloat16 [4, 8192, 1024], P('segment', 'mp'), may hold values from -0.0625 to 0.0625
- w_unit: bfloat16 [1024, 10240], P(None, ('segment', 'mp')), as said below
Outputs:
- loss: float32 [4], P('dp')
- grad_in: float32 [4, 1024, 8192], P('segment', 'dp', 'mp')
- grad_out: float32 [4, 8192, 1024], P('segment', 'mp', 'dp')
- grad_unit: float32 [1024, 10240], P('dp', ('segment', 'mp'))
Inputs may be any that keep to these rules, and one draw needn't show every extreme that they name: Within each micro-batch and each index of dp the 128 durations sum to exactly 512, and one of them equals 16. `w_unit`: entries of order 3 / sqrt(1024) in most columns, some columns much larger.
All inputs are finite; a program needn't handle non-finite values.
Results may differ from a plain program's by a relative error of at most 0.035.
Values may be sent and summed in bfloat16 or wider, within the bound.
A program may use at most 128 MiB of HBM per device.

v0:
```python
import jax
import jax.numpy as jnp
from jax import lax
from jax.sharding import PartitionSpec as P


def shifted(block, axis, distance):
    devices = range(lax.axis_size(axis))
    route = [(i - distance, i) for i in devices if i - distance in devices]
    return lax.ppermute(block, axis, route)


def broadcast(x, axis, root):
    mine = lax.axis_index(axis) == root
    return lax.psum(jnp.where(mine, x, jnp.zeros_like(x)), axis)


def gelu_parts(pre_vals):
    coeff = 0.7978845608
    inner = coeff * (pre_vals + 0.044715 * pre_vals * pre_vals * pre_vals)
    tanh_val = jnp.tanh(inner)
    value = 0.5 * pre_vals * (1.0 + tanh_val)
    slope = 0.5 * (1.0 + tanh_val) + 0.5 * pre_vals * (1.0 - tanh_val * tanh_val) * coeff * (
        1.0 + 3.0 * 0.044715 * pre_vals * pre_vals
    )
    return (value, slope)


def row_scale(rows_in):
    floats = rows_in.astype(jnp.float32)
    return lax.rsqrt(jnp.mean(floats * floats, axis=-1, keepdims=True) + 1e-06)


def norm_back(rows_in, grads):
    scale = row_scale(rows_in)
    normal = rows_in.astype(jnp.float32) * scale
    return scale * (grads - normal * jnp.mean(grads * normal, axis=-1, keepdims=True))


def section(rows_in, first):
    normed = (rows_in.astype(jnp.float32) * row_scale(rows_in)).astype(jnp.bfloat16)
    pre_vals = jnp.dot(normed, first, preferred_element_type=jnp.float32)
    value, slope = gelu_parts(pre_vals)
    return (normed, value.astype(jnp.bfloat16), slope)


def finish_forward(pieces, summed):
    return (pieces[0].astype(jnp.float32) + summed).astype(jnp.bfloat16)


def finish_backward(pieces, summed):
    return (pieces[0].astype(jnp.float32) + norm_back(pieces[1], summed)).astype(jnp.bfloat16)


def reduce_rows(partial_value, pieces, finisher):
    summed = lax.psum(partial_value, "mp")
    return finisher(pieces, summed)


def on_device(text_rows, durations, unit_targets, w_in, w_out, w_unit):
    micro_count, row_count, width = text_rows.shape
    segments = lax.axis_size("segment")
    segment_at = lax.axis_index("segment")
    first = w_in[0]
    second = w_out[0]
    clocks = micro_count + segments - 1
    stash = jnp.zeros((micro_count, row_count, width), jnp.bfloat16)
    final_rows = jnp.zeros((micro_count, row_count, width), jnp.bfloat16)
    outgoing = jnp.zeros((row_count, width), jnp.bfloat16)
    for clock in range(clocks):
        if clock > 0:
            incoming = shifted(outgoing, "segment", 1)
        else:
            incoming = jnp.zeros((row_count, width), jnp.bfloat16)
        rows_in = jnp.where(segment_at == 0, text_rows[min(clock, micro_count - 1)], incoming)
        batch_at = clock - segment_at
        is_live = (batch_at >= 0) & (batch_at < micro_count)
        slot_at = jnp.clip(batch_at, 0, micro_count - 1)
        stash = jnp.where(
            is_live, lax.dynamic_update_index_in_dim(stash, rows_in, slot_at, 0), stash
        )
        normed, hidden, slope = section(rows_in, first)
        partial_value = jnp.dot(hidden, second, preferred_element_type=jnp.float32)
        outgoing = reduce_rows(partial_value, (rows_in,), finish_forward)
        is_last = is_live & (segment_at == segments - 1)
        final_rows = jnp.where(
            is_last, lax.dynamic_update_index_in_dim(final_rows, outgoing, slot_at, 0), final_rows
        )
    final_rows = broadcast(final_rows, "segment", segments - 1)
    vocab_part = w_unit.shape[1]
    vocab_start = lax.axis_index(("segment", "mp")) * vocab_part
    final_norm = (final_rows.astype(jnp.float32) * row_scale(final_rows)).astype(jnp.bfloat16)
    logits = jnp.einsum("mrd,dv->mrv", final_norm, w_unit, preferred_element_type=jnp.float32)
    lengths = durations[:, 0, :]
    unit_count = unit_targets.shape[1]
    ends = jnp.cumsum(lengths, axis=-1)
    positions = jnp.arange(unit_count, dtype=jnp.int32)
    row_local = jnp.sum((ends[:, None, :] <= positions[None, :, None]).astype(jnp.int32), axis=-1)
    row_onehot = (
        row_local[:, :, None] == jnp.arange(row_count, dtype=jnp.int32)[None, None, :]
    ).astype(jnp.bfloat16)
    vocab_ids = vocab_start + jnp.arange(vocab_part, dtype=jnp.int32)
    target_hits = (unit_targets[:, :, None] == vocab_ids[None, None, :]).astype(jnp.bfloat16)
    counts = jnp.einsum("mur,muv->mrv", row_onehot, target_hits, preferred_element_type=jnp.float32)
    local_peak = jnp.max(logits, axis=-1)
    target_local = jnp.sum(counts * logits, axis=-1)
    peak = lax.pmax(local_peak, ("segment", "mp"))
    total, target_sum = lax.psum(
        (jnp.sum(jnp.exp(logits - peak[..., None]), axis=-1), target_local), ("segment", "mp")
    )
    lse = peak + jnp.log(total)
    denom = float(micro_count * unit_count * lax.axis_size("dp"))
    length_f = lengths.astype(jnp.float32)
    loss_local = jnp.sum(length_f * lse - target_sum)
    loss = (loss_local / denom)[None]
    dlogits = ((length_f[..., None] * jnp.exp(logits - lse[..., None]) - counts) / denom).astype(
        jnp.bfloat16
    )
    grad_unit = jnp.einsum("mrd,mrv->dv", final_norm, dlogits, preferred_element_type=jnp.float32)
    norm_part = jnp.einsum("mrv,dv->mrd", dlogits, w_unit, preferred_element_type=jnp.float32)
    norm_share = lax.psum_scatter(
        norm_part, ("segment", "mp"), scatter_dimension=2, tiled=True
    ).astype(jnp.bfloat16)
    dnorm = lax.all_gather(norm_share, ("segment", "mp"), axis=2, tiled=True)
    grad_final = norm_back(final_rows, dnorm.astype(jnp.float32)).astype(jnp.bfloat16)
    grad_first = jnp.zeros(first.shape, jnp.float32)
    grad_second = jnp.zeros(second.shape, jnp.float32)
    going_back = jnp.zeros((row_count, width), jnp.bfloat16)
    for clock in range(clocks):
        if clock > 0:
            arriving = shifted(going_back, "segment", -1)
        else:
            arriving = jnp.zeros((row_count, width), jnp.bfloat16)
        grad_rows = jnp.where(
            segment_at == segments - 1, grad_final[min(clock, micro_count - 1)], arriving
        )
        batch_at = clock - (segments - 1 - segment_at)
        is_live = (batch_at >= 0) & (batch_at < micro_count)
        slot_at = jnp.clip(batch_at, 0, micro_count - 1)
        rows_in = lax.dynamic_index_in_dim(stash, slot_at, 0, keepdims=False)
        normed, hidden, slope = section(rows_in, first)
        live_f = is_live.astype(jnp.float32)
        grad_second = grad_second + live_f * jnp.dot(
            hidden.T, grad_rows, preferred_element_type=jnp.float32
        )
        dhidden = jnp.dot(grad_rows, second.T, preferred_element_type=jnp.float32)
        dpre = (dhidden * slope).astype(jnp.bfloat16)
        grad_first = grad_first + live_f * jnp.dot(
            normed.T, dpre, preferred_element_type=jnp.float32
        )
        dnormed = jnp.dot(dpre, first.T, preferred_element_type=jnp.float32)
        going_back = reduce_rows(dnormed, (grad_rows, rows_in), finish_backward)
    sum_first, sum_second, sum_unit = (
        lax.psum_scatter(grad_first, "dp", scatter_dimension=0, tiled=True),
        lax.psum_scatter(grad_second, "dp", scatter_dimension=1, tiled=True),
        lax.psum_scatter(grad_unit, "dp", scatter_dimension=0, tiled=True),
    )
    return (loss, sum_first[None], sum_second[None], sum_unit)


def solution(mesh):
    placed = (
        P(None, "dp", None),
        P(None, "dp", None),
        P(None, "dp"),
        P("segment", None, "mp"),
        P("segment", "mp", None),
        P(None, ("segment", "mp")),
    )
    return jax.shard_map(
        on_device,
        mesh=mesh,
        in_specs=placed,
        out_specs=(
            P("dp"),
            P("segment", "dp", "mp"),
            P("segment", "mp", "dp"),
            P("dp", ("segment", "mp")),
        ),
        check_vma=False,
    )
```

profile of v0, /device:TPU:1, one launch (start us, length us, event | category | flops | bytes accessed | tf_op | source)
XLA Modules:
  0.0 2379.7 jit_solution(6565013018614124377)
XLA Ops:
  11.3 113.5 %all-reduce.18.cloned.1.call-done = f32[128,1024]{1,0:T(8,128)} async-done(((f32[128,1024]{1,0:T(8,128)}), f32[128,1024]{1,0:T(8,128)}) %all-reduce.18.cloned.1.call-update) | async-done | bytes 524304 | tf_op jit(solution)/shard_map/psum | solution.py:56
  137.0 111.0 %all-reduce.20.cloned.1.call-done = f32[128,1024]{1,0:T(8,128)} async-done(((f32[128,1024]{1,0:T(8,128)}), f32[128,1024]{1,0:T(8,128)}) %all-reduce.20.cloned.1.call-update) | async-done | bytes 524304 | tf_op jit(solution)/shard_map/psum | solution.py:56
  253.2 5.2 collective-permute-done.1
  261.9 110.8 %all-reduce.22.cloned.1.call-done = f32[128,1024]{1,0:T(8,128)} async-done(((f32[128,1024]{1,0:T(8,128)}), f32[128,1024]{1,0:T(8,128)}) %all-reduce.22.cloned.1.call-update) | async-done | bytes 524304 | tf_op jit(solution)/shard_map/psum | solution.py:56
  377.8 5.2 collective-permute-done.2
  386.5 110.8 %all-reduce.24.cloned.1.call-done = f32[128,1024]{1,0:T(8,128)} async-done(((f32[128,1024]{1,0:T(8,128)}), f32[128,1024]{1,0:T(8,128)}) %all-reduce.24.cloned.1.call-update) | async-done | bytes 524304 | tf_op jit(solution)/shard_map/psum | solution.py:56
  502.4 5.2 collective-permute-done.3
  511.1 110.8 %all-reduce.26.cloned.1.call-done = f32[128,1024]{1,0:T(8,128)} async-done(((f32[128,1024]{1,0:T(8,128)}), f32[128,1024]{1,0:T(8,128)}) %all-reduce.26.cloned.1.call-update) | async-done | bytes 524304 | tf_op jit(solution)/shard_map/psum | solution.py:56
  627.0 5.2 collective-permute-done.4
  635.7 110.8 %all-reduce.28.cloned.1.call-done = f32[128,1024]{1,0:T(8,128)} async-done(((f32[128,1024]{1,0:T(8,128)}), f32[128,1024]{1,0:T(8,128)}) %all-reduce.28.cloned.1.call-update) | async-done | bytes 524304 | tf_op jit(solution)/shard_map/psum | solution.py:56
  760.3 110.8 %all-reduce.30.cloned.1.call-done = f32[128,1024]{1,0:T(8,128)} async-done(((f32[128,1024]{1,0:T(8,128)}), f32[128,1024]{1,0:T(8,128)}) %all-reduce.30.cloned.1.call-update) | async-done | bytes 524304 | tf_op jit(solution)/shard_map/psum | solution.py:56
  876.2 49.1 %all-reduce.32.cloned.1.call-done = bf16[4,128,1024]{2,1,0:T(8,128)(2,1)} async-done(((bf16[4,128,1024]{2,1,0:T(8,128)(2,1)}), bf16[4,128,1024]{2,1,0:T(8,128)(2,1)}) %all-reduce.32.cloned.1.call-update) | async-done | bytes 1048592 | tf_op jit(solution)/shard_map/psum | solution.py:15
  929.3 125.5 %pmax.7 = f32[4,128]{1,0:T(4,128)S(1)} all-reduce(f32[4,128]{1,0:T(4,128)S(1)} %get-tuple-element.40), channel_id=1, replica_groups=mesh['segment'=4,'mp'=16,'dp'=4] {'segment','mp'}, use_global_device_ids=true, to_apply=%region_17.18 | all-reduce | flops 512 | bytes 4096 | tf_op jit(solution)/shard_map/pmax | solution.py:107
  1057.1 127.1 %psum.120 = f32[4,128]{1,0:T(4,128)S(1)} all-reduce(f32[4,128]{1,0:T(4,128)S(1)} %get-tuple-element.12), channel_id=1, replica_groups=mesh['segment'=4,'mp'=16,'dp'=4] {'segment','mp'}, use_global_device_ids=true, to_apply=%region_19.20 | all-reduce | flops 512 | bytes 4096 | tf_op jit(solution)/shard_map/psum | solution.py:108
  1189.2 265.5 %all-reduce.45 = (f32[4,128]{1,0:T(4,128)}, bf16[4,128,1024]{1,0,2:T(4,128)(2,1)}) all-reduce(f32[4,128]{1,0:T(4,128)S(1)} %get-tuple-element.13, f32[4,128,1024]{1,0,2:T(4,128)} %copy.13), channel_id=1, replica_groups=mesh['segment'=4,'mp'=16,'dp'=4] {'segment','mp'}, use_global_device_ids=true, to_apply=%region_23.24 | all-reduce | flops 524800 | bytes 3149824 | tf_op jit(solution)/shard_map/psum | solution.py:108
  1456.9 75.1 %all-gather.2.cloned.1.call-done = bf16[4,128,1024]{1,0,2:T(4,128)(2,1)} async-done(((bf16[4,128,16]{1,0,2:T(4,128)(2,1)}), bf16[4,128,1024]{1,0,2:T(4,128)(2,1)}) %all-gather.2.cloned.1.call-update) | async-done | bytes 1048592 | tf_op jit(solution)/shard_map/all_gather | solution.py:124
  1540.1 106.9 %all-reduce.34.cloned.1.call-done = f32[128,1024]{1,0:T(8,128)} async-done(((f32[128,1024]{1,0:T(8,128)}), f32[128,1024]{1,0:T(8,128)}) %all-reduce.34.cloned.1.call-update) | async-done | bytes 524304 | tf_op jit(solution)/shard_map/psum | solution.py:56
  1651.1 7.3 collective-permute-done.6
  1661.0 109.8 %all-reduce.36.cloned.1.call-done = f32[128,1024]{1,0:T(8,128)} async-done(((f32[128,1024]{1,0:T(8,128)}), f32[128,1024]{1,0:T(8,128)}) %all-reduce.36.cloned.1.call-update) | async-done | bytes 524304 | tf_op jit(solution)/shard_map/psum | solution.py:56
  1775.8 6.7 collective-permute-done.7
  1786.7 109.8 %all-reduce.38.cloned.1.call-done = f32[128,1024]{1,0:T(8,128)} async-done(((f32[128,1024]{1,0:T(8,128)}), f32[128,1024]{1,0:T(8,128)}) %all-reduce.38.cloned.1.call-update) | async-done | bytes 524304 | tf_op jit(solution)/shard_map/psum | solution.py:56
  1901.5 6.7 collective-permute-done.8
  1912.4 109.8 %all-reduce.40.cloned.1.call-done = f32[128,1024]{1,0:T(8,128)} async-done(((f32[128,1024]{1,0:T(8,128)}), f32[128,1024]{1,0:T(8,128)}) %all-reduce.40.cloned.1.call-update) | async-done | bytes 524304 | tf_op jit(solution)/shard_map/psum | solution.py:56
  2027.3 6.7 collective-permute-done.9
  2038.2 109.8 %all-reduce.42.cloned.1.call-done = f32[128,1024]{1,0:T(8,128)} async-done(((f32[128,1024]{1,0:T(8,128)}), f32[128,1024]{1,0:T(8,128)}) %all-reduce.42.cloned.1.call-update) | async-done | bytes 524304 | tf_op jit(solution)/shard_map/psum | solution.py:56
  2153.0 6.7 collective-permute-done.10
  2178.9 94.8 %all-reduce.44.cloned.1.call-done = f32[128,1024]{1,0:T(8,128)} async-done(((f32[128,1024]{1,0:T(8,128)}), f32[128,1024]{1,0:T(8,128)}) %all-reduce.44.cloned.1.call-update) | async-done | bytes 524304 | tf_op jit(solution)/shard_map/psum | solution.py:56
  2278.2 7.3 collective-permute-done.11
  2286.2 6.7 multiply_add_fusion
  2305.0 7.7 multiply_add_fusion.1
  2314.6 21.9 reduce-scatter.6.cloned.1.call-done
  2336.6 35.2 %reduce-scatter.4.cloned.1.call-done = f32[256,512]{1,0:T(8,128)} async-done(((f32[1024,512]{1,0:T(8,128)}), f32[256,512]{1,0:T(8,128)}) %reduce-scatter.4.cloned.1.call-update) | async-done | bytes 524304 | tf_op jit(solution)/shard_map/reduce_scatter | solution.py:154
  (293 shorter events, 166.7 us)
Async XLA Ops:
  7.2 117.6 %all-reduce.18.cloned.1.call-start = ((), (), s32[]{:S(2)}) async-start(), calls=%async_computation.3 | async-start | bytes 1048576 | tf_op jit(solution)/shard_map/psum | solution.py:56
  11.2 236.8 %all-reduce.20.cloned.1.call-start = ((), (), s32[]{:S(2)}) async-start(), calls=%async_computation.4 | async-start | bytes 1048576 | tf_op jit(solution)/shard_map/psum | solution.py:56
  126.2 8.0 collective-permute-start
  137.0 235.7 %all-reduce.22.cloned.1.call-start = ((), (), s32[]{:S(2)}) async-start(), calls=%async_computation.5 | async-start | bytes 1048576 | tf_op jit(solution)/shard_map/psum | solution.py:56
  250.1 8.3 collective-permute-start.1
  261.8 235.4 %all-reduce.24.cloned.1.call-start = ((), (), s32[]{:S(2)}) async-start(), calls=%async_computation.6 | async-start | bytes 1048576 | tf_op jit(solution)/shard_map/psum | solution.py:56
  374.7 8.3 collective-permute-start.2
  386.4 235.4 %all-reduce.26.cloned.1.call-start = ((), (), s32[]{:S(2)}) async-start(), calls=%async_computation.7 | async-start | bytes 1048576 | tf_op jit(solution)/shard_map/psum | solution.py:56
  499.3 8.3 collective-permute-start.3
  511.0 235.4 %all-reduce.28.cloned.1.call-start = ((), (), s32[]{:S(2)}) async-start(), calls=%async_computation.8 | async-start | bytes 1048576 | tf_op jit(solution)/shard_map/psum | solution.py:56
  623.9 8.3 collective-permute-start.4
  635.7 235.4 %all-reduce.30.cloned.1.call-start = ((), (), s32[]{:S(2)}) async-start(), calls=%async_computation.9 | async-start | bytes 1048576 | tf_op jit(solution)/shard_map/psum | solution.py:56
  748.5 8.3 collective-permute-start.5
  760.3 165.0 %all-reduce.32.cloned.1.call-start = ((), (), s32[]{:S(2)}) async-start(), calls=%async_computation.10 | async-start | bytes 2097152 | tf_op jit(solution)/shard_map/psum | solution.py:15
  874.2 180.6 %copy-start.59 = (s32[4,512]{1,0:T(4,128)S(1)}, s32[4,512]{1,0:T(4,128)}, u32[]{:S(2)}) copy-start(s32[4,512]{1,0:T(4,128)} %param.8) | copy-start | bytes 24580
  874.2 657.7 %all-gather.2.cloned.1.call-start = ((), (), s32[]{:S(2)}) async-start(), calls=%async_computation.11 | async-start | bytes 1064960 | tf_op jit(solution)/shard_map/all_gather | solution.py:124
  1456.1 190.9 %all-reduce.34.cloned.1.call-start = ((), (), s32[]{:S(2)}) async-start(), calls=%async_computation.12 | async-start | bytes 1048576 | tf_op jit(solution)/shard_map/psum | solution.py:56
  1456.5 192.7 %copy-start.55 = (f32[128]{0:T(128)}, f32[128]{0:T(128)S(1)}, u32[]{:S(2)}) copy-start(f32[128]{0:T(128)S(1)} %add_rsqrt_fusion.7) | copy-start | bytes 1540
  1540.0 230.8 %all-reduce.36.cloned.1.call-start = ((), (), s32[]{:S(2)}) async-start(), calls=%async_computation.13 | async-start | bytes 1048576 | tf_op jit(solution)/shard_map/psum | solution.py:56
  1649.4 9.0 collective-permute-start.6
  1661.0 235.5 %all-reduce.38.cloned.1.call-start = ((), (), s32[]{:S(2)}) async-start(), calls=%async_computation.14 | async-start | bytes 1048576 | tf_op jit(solution)/shard_map/psum | solution.py:56
  1773.4 9.0 collective-permute-start.7
  1786.6 235.6 %all-reduce.40.cloned.1.call-start = ((), (), s32[]{:S(2)}) async-start(), calls=%async_computation.15 | async-start | bytes 1048576 | tf_op jit(solution)/shard_map/psum | solution.py:56
  1899.1 9.0 collective-permute-start.8
  1912.4 235.6 %all-reduce.42.cloned.1.call-start = ((), (), s32[]{:S(2)}) async-start(), calls=%async_computation.16 | async-start | bytes 1048576 | tf_op jit(solution)/shard_map/psum | solution.py:56
  2024.9 9.0 collective-permute-start.9
  2038.1 235.6 %all-reduce.44.cloned.1.call-start = ((), (), s32[]{:S(2)}) async-start(), calls=%async_computation.17 | async-start | bytes 1048576 | tf_op jit(solution)/shard_map/psum | solution.py:56
  2150.7 9.0 collective-permute-start.10
  2163.9 150.7 %reduce-scatter.8.cloned.1.call-start = ((), (), s32[]{:S(2)}) async-start(), calls=%async_computation.20 | async-start | bytes 819200 | tf_op jit(solution)/shard_map/reduce_scatter | solution.py:156
  2166.6 169.9 %reduce-scatter.6.cloned.1.call-start = ((), (), s32[]{:S(2)}) async-start(), calls=%async_computation.19 | async-start | bytes 2621440 | tf_op jit(solution)/shard_map/reduce_scatter | solution.py:155
  2276.5 9.0 collective-permute-start.11
  2292.9 78.8 %reduce-scatter.4.cloned.1.call-start = ((), (), s32[]{:S(2)}) async-start(), calls=%async_computation.18 | async-start | bytes 2621440 | tf_op jit(solution)/shard_map/reduce_scatter | solution.py:154
  (59 other events, 808.3 us)
Sparse Core Ops, SparseCore 0:
  11.4 113.3 all-reduce.17
  137.1 110.8 all-reduce.19
  261.9 110.6 all-reduce.21
  386.5 110.6 all-reduce.23
  511.2 110.6 all-reduce.25
  635.8 110.6 all-reduce.27
  760.4 110.6 all-reduce.29
  874.3 50.9 all-reduce.31
  1456.2 75.6 all-gather.1
  1540.1 106.8 all-reduce.33
  1661.1 109.7 all-reduce.35
  1786.8 109.7 all-reduce.37
  1912.5 109.7 all-reduce.39
  2038.3 109.7 all-reduce.41
  2164.0 109.6 all-reduce.43
  2276.7 23.4 reduce-scatter.7
  2303.2 33.2 reduce-scatter.5
  2339.7 31.9 reduce-scatter.3
where the time goes:
time: 2380 us
  waiting for transfers between devices  1670 us (70%)
  blocking collectives  518 us (22%)
  matrix products  70.9 us (3%)
  other arithmetic  53.3 us (2%)
  starting transfers between devices  28.3 us (1%)
    psum x13, waiting for transfers between devices, reduce_rows(): summed = lax.psum(partial_value, 'mp')  1420 us
    psum x2, blocking collectives, on_device(): lax.psum((jnp.sum(jnp.exp(logits - peak[..., None]), axis=-1), target_loc...  393 us
    pmax x1, blocking collectives, on_device(): peak = lax.pmax(local_peak, ('segment', 'mp'))  125 us
    all_gather x1, waiting for transfers between devices, on_device(): dnorm = lax.all_gather(norm_share, ('segment', 'mp'), axis=2, tiled=True)  75.1 us
    ppermute x12, waiting for transfers between devices, shifted(): return lax.ppermute(block, axis, route)  70.4 us
    psum x1, waiting for transfers between devices, broadcast(): return lax.psum(jnp.where(mine, x, jnp.zeros_like(x)), axis)  49.1 us
  transfers between devices with their start and end apart: 30, of which 29 were waited for; matrix products, arithmetic and copies ran while one was open for 2% of the time, Pallas kernels for 0%

commit v1 on v0

--- a/solution.py
+++ b/solution.py
@@ -1,7 +1,17 @@
+import functools
 import jax
 import jax.numpy as jnp
 from jax import lax
 from jax.sharding import PartitionSpec as P
+
+
+def spread_sums_all(t0, a_name, across):
+    for s in (a_name, across):
+        t0 = lax.psum(t0, axis_name=s)
+    return t0
+
+
+pair_the_samples = functools.partial(spread_sums_all, a_name="segment", across="mp")
 
 
 def shifted(block, axis, distance):
@@ -105,8 +115,8 @@
     local_peak = jnp.max(logits, axis=-1)
     target_local = jnp.sum(counts * logits, axis=-1)
     peak = lax.pmax(local_peak, ("segment", "mp"))
-    total, target_sum = lax.psum(
-        (jnp.sum(jnp.exp(logits - peak[..., None]), axis=-1), target_local), ("segment", "mp")
+    total, target_sum = pair_the_samples(
+        (jnp.sum(jnp.exp(logits - peak[..., None]), axis=-1), target_local)
     )
     lse = peak + jnp.log(total)
     denom = float(micro_count * unit_count * lax.axis_size("dp"))

time: 2380 us -> 2290 us (0.962)
  blocking collectives: 518 us -> 423 us
    psum x2, blocking collectives: 393 us -> 34.3 us  [spread_sums_all(): t0 = lax.psum(t0, axis_name=s)]
    unnamed x0 -> x1, blocking collectives: none -> 263 us
where the time goes in v1:
time: 2290 us; the launch traced here: 2280 us
  waiting for transfers between devices  1670 us (73%)
  blocking collectives  423 us (18%)
  matrix products  70.2 us (3%)
  other arithmetic  53.2 us (2%)
  starting transfers between devices  28.3 us (1%)
    psum x13, waiting for transfers between devices, reduce_rows(): summed = lax.psum(partial_value, 'mp')  1420 us
    unnamed x1, blocking collectives  263 us
    pmax x1, blocking collectives, on_device(): peak = lax.pmax(local_peak, ('segment', 'mp'))  125 us
    all_gather x1, waiting for transfers between devices, on_device(): dnorm = lax.all_gather(norm_share, ('segment', 'mp'), axis=2, tiled=True)  75 us
    ppermute x12, waiting for transfers between devices, shifted(): return lax.ppermute(block, axis, route)  70.6 us
    psum x1, waiting for transfers between devices, broadcast(): return lax.psum(jnp.where(mine, x, jnp.zeros_like(x)), axis)  49.1 us
  transfers between devices with their start and end apart: 30, of which 29 were waited for; matrix products, arithmetic and copies ran while one was open for 2% of the time, Pallas kernels for 0%

profile of v1, /device:TPU:1, one launch (start us, length us, event | category | flops | bytes accessed | tf_op | source)
XLA Modules:
  0.0 2285.0 jit_solution(3971366425841515006)
XLA Ops:
  11.3 113.5 %all-reduce.19.cloned.1.call-done = f32[128,1024]{1,0:T(8,128)} async-done(((f32[128,1024]{1,0:T(8,128)}), f32[128,1024]{1,0:T(8,128)}) %all-reduce.19.cloned.1.call-update) | async-done | bytes 524304 | tf_op jit(solution)/shard_map/psum | solution.py:66
  137.0 111.0 %all-reduce.21.cloned.1.call-done = f32[128,1024]{1,0:T(8,128)} async-done(((f32[128,1024]{1,0:T(8,128)}), f32[128,1024]{1,0:T(8,128)}) %all-reduce.21.cloned.1.call-update) | async-done | bytes 524304 | tf_op jit(solution)/shard_map/psum | solution.py:66
  253.2 5.2 collective-permute-done.1
  261.9 110.8 %all-reduce.23.cloned.1.call-done = f32[128,1024]{1,0:T(8,128)} async-done(((f32[128,1024]{1,0:T(8,128)}), f32[128,1024]{1,0:T(8,128)}) %all-reduce.23.cloned.1.call-update) | async-done | bytes 524304 | tf_op jit(solution)/shard_map/psum | solution.py:66
  377.8 5.2 collective-permute-done.2
  386.5 110.8 %all-reduce.25.cloned.1.call-done = f32[128,1024]{1,0:T(8,128)} async-done(((f32[128,1024]{1,0:T(8,128)}), f32[128,1024]{1,0:T(8,128)}) %all-reduce.25.cloned.1.call-update) | async-done | bytes 524304 | tf_op jit(solution)/shard_map/psum | solution.py:66
  511.1 110.8 %all-reduce.27.cloned.1.call-done = f32[128,1024]{1,0:T(8,128)} async-done(((f32[128,1024]{1,0:T(8,128)}), f32[128,1024]{1,0:T(8,128)}) %all-reduce.27.cloned.1.call-update) | async-done | bytes 524304 | tf_op jit(solution)/shard_map/psum | solution.py:66
  635.7 110.8 %all-reduce.29.cloned.1.call-done = f32[128,1024]{1,0:T(8,128)} async-done(((f32[128,1024]{1,0:T(8,128)}), f32[128,1024]{1,0:T(8,128)}) %all-reduce.29.cloned.1.call-update) | async-done | bytes 524304 | tf_op jit(solution)/shard_map/psum | solution.py:66
  751.7 5.2 collective-permute-done.5
  760.4 110.8 %all-reduce.31.cloned.1.call-done = f32[128,1024]{1,0:T(8,128)} async-done(((f32[128,1024]{1,0:T(8,128)}), f32[128,1024]{1,0:T(8,128)}) %all-reduce.31.cloned.1.call-update) | async-done | bytes 524304 | tf_op jit(solution)/shard_map/psum | solution.py:66
  876.2 49.1 %all-reduce.33.cloned.1.call-done = bf16[4,128,1024]{2,1,0:T(8,128)(2,1)} async-done(((bf16[4,128,1024]{2,1,0:T(8,128)(2,1)}), bf16[4,128,1024]{2,1,0:T(8,128)(2,1)}) %all-reduce.33.cloned.1.call-update) | async-done | bytes 1048592 | tf_op jit(solution)/shard_map/psum | solution.py:25
  929.4 125.5 %pmax.7 = f32[4,128]{1,0:T(4,128)S(1)} all-reduce(f32[4,128]{1,0:T(4,128)S(1)} %get-tuple-element.44), channel_id=1, replica_groups=mesh['segment'=4,'mp'=16,'dp'=4] {'segment','mp'}, use_global_device_ids=true, to_apply=%region_17.18 | all-reduce | flops 512 | bytes 4096 | tf_op jit(solution)/shard_map/pmax | solution.py:117
  1057.1 6.0 all-reduce.2
  1063.1 28.3 %all-reduce.1 = (f32[4,128]{1,0:T(4,128)S(1)}, f32[4,128]{1,0:T(4,128)S(1)}) all-reduce(f32[4,128]{1,0:T(4,128)S(1)} %get-tuple-element.16, f32[4,128]{1,0:T(4,128)S(1)} %get-tuple-element.17), channel_id=1, replica_groups=mesh['segment'=4,'mp'=16,'dp'=4] {'mp'}, use_global_device_ids=true, to_apply=%region_25.26 | all-reduce | flops 1024 | bytes 8192 | tf_op jit(solution)/shard_map/psum | solution.py:10
  1097.1 263.5 %all-reduce.46 = bf16[4,128,1024]{1,0,2:T(4,128)(2,1)} all-reduce(f32[4,128,1024]{1,0,2:T(4,128)} %copy.13), channel_id=2, replica_groups=mesh['segment'=4,'mp'=16,'dp'=4] {'segment','mp'}, use_global_device_ids=true, to_apply=%region_28.29.clone | all-reduce | flops 524288 | bytes 3145728
  1362.7 75.0 %all-gather.2.cloned.1.call-done = bf16[4,128,1024]{1,0,2:T(4,128)(2,1)} async-done(((bf16[4,128,16]{1,0,2:T(4,128)(2,1)}), bf16[4,128,1024]{1,0,2:T(4,128)(2,1)}) %all-gather.2.cloned.1.call-update) | async-done | bytes 1048592 | tf_op jit(solution)/shard_map/all_gather | solution.py:134
  1445.8 106.8 %all-reduce.35.cloned.1.call-done = f32[128,1024]{1,0:T(8,128)} async-done(((f32[128,1024]{1,0:T(8,128)}), f32[128,1024]{1,0:T(8,128)}) %all-reduce.35.cloned.1.call-update) | async-done | bytes 524304 | tf_op jit(solution)/shard_map/psum | solution.py:66
  1556.6 7.3 collective-permute-done.6
  1566.6 109.8 %all-reduce.37.cloned.1.call-done = f32[128,1024]{1,0:T(8,128)} async-done(((f32[128,1024]{1,0:T(8,128)}), f32[128,1024]{1,0:T(8,128)}) %all-reduce.37.cloned.1.call-update) | async-done | bytes 524304 | tf_op jit(solution)/shard_map/psum | solution.py:66
  1681.3 6.7 collective-permute-done.7
  1692.2 109.6 %all-reduce.39.cloned.1.call-done = f32[128,1024]{1,0:T(8,128)} async-done(((f32[128,1024]{1,0:T(8,128)}), f32[128,1024]{1,0:T(8,128)}) %all-reduce.39.cloned.1.call-update) | async-done | bytes 524304 | tf_op jit(solution)/shard_map/psum | solution.py:66
  1806.8 6.7 collective-permute-done.8
  1817.7 109.8 %all-reduce.41.cloned.1.call-done = f32[128,1024]{1,0:T(8,128)} async-done(((f32[128,1024]{1,0:T(8,128)}), f32[128,1024]{1,0:T(8,128)}) %all-reduce.41.cloned.1.call-update) | async-done | bytes 524304 | tf_op jit(solution)/shard_map/psum | solution.py:66
  1932.5 6.8 collective-permute-done.9
  1943.5 109.8 %all-reduce.43.cloned.1.call-done = f32[128,1024]{1,0:T(8,128)} async-done(((f32[128,1024]{1,0:T(8,128)}), f32[128,1024]{1,0:T(8,128)}) %all-reduce.43.cloned.1.call-update) | async-done | bytes 524304 | tf_op jit(solution)/shard_map/psum | solution.py:66
  2058.3 6.7 collective-permute-done.10
  2084.2 94.8 %all-reduce.45.cloned.1.call-done = f32[128,1024]{1,0:T(8,128)} async-done(((f32[128,1024]{1,0:T(8,128)}), f32[128,1024]{1,0:T(8,128)}) %all-reduce.45.cloned.1.call-update) | async-done | bytes 524304 | tf_op jit(solution)/shard_map/psum | solution.py:66
  2183.4 7.3 collective-permute-done.11
  2191.5 6.7 multiply_add_fusion
  2210.1 7.7 multiply_add_fusion.1
  2218.5 23.4 %reduce-scatter.6.cloned.1.call-done = f32[512,256]{1,0:T(8,128)} async-done(((f32[512,1024]{1,0:T(8,128)}), f32[512,256]{1,0:T(8,128)}) %reduce-scatter.6.cloned.1.call-update) | async-done | bytes 524304 | tf_op jit(solution)/shard_map/reduce_scatter | solution.py:165
  2241.8 35.2 %reduce-scatter.4.cloned.1.call-done = f32[256,512]{1,0:T(8,128)} async-done(((f32[1024,512]{1,0:T(8,128)}), f32[256,512]{1,0:T(8,128)}) %reduce-scatter.4.cloned.1.call-update) | async-done | bytes 524304 | tf_op jit(solution)/shard_map/reduce_scatter | solution.py:164
  (285 shorter events, 170.9 us)
Async XLA Ops:
  7.2 117.6 %all-reduce.19.cloned.1.call-start = ((), (), s32[]{:S(2)}) async-start(), calls=%async_computation.3 | async-start | bytes 1048576 | tf_op jit(solution)/shard_map/psum | solution.py:66
  11.2 236.8 %all-reduce.21.cloned.1.call-start = ((), (), s32[]{:S(2)}) async-start(), calls=%async_computation.4 | async-start | bytes 1048576 | tf_op jit(solution)/shard_map/psum | solution.py:66
  126.2 8.0 collective-permute-start
  137.0 235.7 %all-reduce.23.cloned.1.call-start = ((), (), s32[]{:S(2)}) async-start(), calls=%async_computation.5 | async-start | bytes 1048576 | tf_op jit(solution)/shard_map/psum | solution.py:66
  250.1 8.3 collective-permute-start.1
  261.8 235.4 %all-reduce.25.cloned.1.call-start = ((), (), s32[]{:S(2)}) async-start(), calls=%async_computation.6 | async-start | bytes 1048576 | tf_op jit(solution)/shard_map/psum | solution.py:66
  374.7 8.3 collective-permute-start.2
  386.4 235.4 %all-reduce.27.cloned.1.call-start = ((), (), s32[]{:S(2)}) async-start(), calls=%async_computation.7 | async-start | bytes 1048576 | tf_op jit(solution)/shard_map/psum | solution.py:66
  499.3 8.3 collective-permute-start.3
  511.1 235.5 %all-reduce.29.cloned.1.call-start = ((), (), s32[]{:S(2)}) async-start(), calls=%async_computation.8 | async-start | bytes 1048576 | tf_op jit(solution)/shard_map/psum | solution.py:66
  623.9 8.3 collective-permute-start.4
  635.7 235.5 %all-reduce.31.cloned.1.call-start = ((), (), s32[]{:S(2)}) async-start(), calls=%async_computation.9 | async-start | bytes 1048576 | tf_op jit(solution)/shard_map/psum | solution.py:66
  748.6 8.3 collective-permute-start.5
  760.3 165.0 %all-reduce.33.cloned.1.call-start = ((), (), s32[]{:S(2)}) async-start(), calls=%async_computation.10 | async-start | bytes 2097152 | tf_op jit(solution)/shard_map/psum | solution.py:25
  874.2 180.6 %copy-start.55 = (s32[4,512]{1,0:T(4,128)S(1)}, s32[4,512]{1,0:T(4,128)}, u32[]{:S(2)}) copy-start(s32[4,512]{1,0:T(4,128)} %param.8) | copy-start | bytes 24580
  874.2 563.5 %all-gather.2.cloned.1.call-start = ((), (), s32[]{:S(2)}) async-start(), calls=%async_computation.11 | async-start | bytes 1064960 | tf_op jit(solution)/shard_map/all_gather | solution.py:134
  1361.9 190.6 %all-reduce.35.cloned.1.call-start = ((), (), s32[]{:S(2)}) async-start(), calls=%async_computation.12 | async-start | bytes 1048576 | tf_op jit(solution)/shard_map/psum | solution.py:66
  1362.3 192.4 %copy-start.51 = (f32[128]{0:T(128)}, f32[128]{0:T(128)S(1)}, u32[]{:S(2)}) copy-start(f32[128]{0:T(128)S(1)} %add_rsqrt_fusion.7) | copy-start | bytes 1540
  1445.7 230.7 %all-reduce.37.cloned.1.call-start = ((), (), s32[]{:S(2)}) async-start(), calls=%async_computation.13 | async-start | bytes 1048576 | tf_op jit(solution)/shard_map/psum | solution.py:66
  1555.0 9.0 collective-permute-start.6
  1566.5 235.3 %all-reduce.39.cloned.1.call-start = ((), (), s32[]{:S(2)}) async-start(), calls=%async_computation.14 | async-start | bytes 1048576 | tf_op jit(solution)/shard_map/psum | solution.py:66
  1679.0 9.0 collective-permute-start.7
  1692.2 235.4 %all-reduce.41.cloned.1.call-start = ((), (), s32[]{:S(2)}) async-start(), calls=%async_computation.15 | async-start | bytes 1048576 | tf_op jit(solution)/shard_map/psum | solution.py:66
  1804.5 9.0 collective-permute-start.8
  1817.7 235.6 %all-reduce.43.cloned.1.call-start = ((), (), s32[]{:S(2)}) async-start(), calls=%async_computation.16 | async-start | bytes 1048576 | tf_op jit(solution)/shard_map/psum | solution.py:66
  1930.2 9.0 collective-permute-start.9
  1943.4 235.6 %all-reduce.45.cloned.1.call-start = ((), (), s32[]{:S(2)}) async-start(), calls=%async_computation.17 | async-start | bytes 1048576 | tf_op jit(solution)/shard_map/psum | solution.py:66
  2055.9 9.0 collective-permute-start.10
  2069.2 149.3 %reduce-scatter.8.cloned.1.call-start = ((), (), s32[]{:S(2)}) async-start(), calls=%async_computation.20 | async-start | bytes 819200 | tf_op jit(solution)/shard_map/reduce_scatter | solution.py:166
  2071.9 170.0 %reduce-scatter.6.cloned.1.call-start = ((), (), s32[]{:S(2)}) async-start(), calls=%async_computation.19 | async-start | bytes 2621440 | tf_op jit(solution)/shard_map/reduce_scatter | solution.py:165
  2181.8 9.0 collective-permute-start.11
  2198.2 78.8 %reduce-scatter.4.cloned.1.call-start = ((), (), s32[]{:S(2)}) async-start(), calls=%async_computation.18 | async-start | bytes 2621440 | tf_op jit(solution)/shard_map/reduce_scatter | solution.py:164
  (55 other events, 548.5 us)
Sparse Core Ops, SparseCore 0:
  11.4 113.3 all-reduce.18
  137.1 110.8 all-reduce.20
  261.9 110.6 all-reduce.22
  386.6 110.6 all-reduce.24
  511.2 110.6 all-reduce.26
  635.8 110.6 all-reduce.28
  760.4 110.6 all-reduce.30
  874.4 50.9 all-reduce.32
  1362.0 75.6 all-gather.1
  1445.9 106.6 all-reduce.34
  1566.6 109.7 all-reduce.36
  1692.3 109.5 all-reduce.38
  1817.8 109.7 all-reduce.40
  1943.5 109.7 all-reduce.42
  2069.3 109.7 all-reduce.44
  2182.0 23.4 reduce-scatter.7
  2208.5 33.2 reduce-scatter.5
  2245.0 31.9 reduce-scatter.3
